TPU v7x, 32 devices: a whole 2x2x4 slice. The times are simulated.
32 devices in a mesh: segment: 4 (over y, x), vocab: 8 (over z, core).
Axes of the slice: x: 2, y: 2, z: 4, core: 2. Of those that a mesh axis runs over, the one named last changes fastest.
Arguments:
- trunk_out: bfloat16 [160, 7168], P(None, 'vocab'), may hold values from -12 to 12
- embeds: bfloat16 [164, 7168], P(None, 'vocab'), may hold values from -12 to 12
- token_ids: int32 [164], replicated, may hold values from 0 to 8191
- module_weight: bfloat16 [4, 2, 7168, 7168], P('segment', None, 'vocab'), may hold values from -0.046875 to 0.046875
- hidden_gain: bfloat16 [3, 7168], P(None, 'vocab'), may hold values from 0.25 to 1.75
- embed_gain: bfloat16 [3, 7168], P(None, 'vocab'), may hold values from 0.25 to 1.75
- out_gain: bfloat16 [4, 7168], P('segment'), may hold values from 0.25 to 1.75
- head_weight: bfloat16 [7168, 8192], P('segment', 'vocab'), may hold values from -0.21260502 to 0.21260502
Outputs:
- losses: float32 [4, 160], P('segment')
All inputs are finite; a program needn't handle non-finite values.
Results may differ from a plain program's by a relative error of at most 0.00095.
Values may be sent and summed in bfloat16 or wider, within the bound.
No kernel may reach another device: no remote copies, remote signals or barrier semaphores. Data moves between devices by JAX's collectives and lax.ppermute only.
A program may use at most 128 MiB of HBM per device.

v0:
```python
import jax
import jax.numpy as jnp
from jax import lax
from jax.sharding import PartitionSpec as P

D = 7168
TOK = 160
MICRO = 4


EPSILON = 1e-06


def passed_along(block, axis, distance):
    devices = range(lax.axis_size(axis))
    route = [(i - distance, i) for i in devices if i - distance in devices]
    return lax.ppermute(block, axis, route)


def combined_all(shard, axis, combine):
    everything = jax.tree.map(lambda part: lax.all_gather(part, axis), shard)
    first = jax.tree.map(lambda part: part[0], everything)

    def step(k, so_far):
        return combine(so_far, jax.tree.map(lambda part: part[k], everything))

    return lax.fori_loop(1, lax.axis_size(axis), step, first)


def merge_softmax(earlier, second):
    highest = jnp.maximum(earlier[0], second[0])
    summed = earlier[1] * jnp.exp(earlier[0] - highest) + second[1] * jnp.exp(second[0] - highest)
    return (highest, summed, earlier[2] + second[2])


def per_device(
    trunk_out, embeds, token_ids, module_weight, hidden_gain, embed_gain, out_gain, head_weight
):
    sections = lax.axis_size("segment")
    section = lax.axis_index("segment")
    shard_index = lax.axis_index("vocab")
    local_width = trunk_out.shape[1]
    micro_rows = TOK // MICRO
    vocab_width = head_weight.shape[1]
    depth_count = hidden_gain.shape[0]
    embed_float = embeds.astype(jnp.float32)
    embed_squares = lax.psum(jnp.sum(embed_float * embed_float, axis=1), "vocab")
    embed_scale = lax.rsqrt(embed_squares / D + EPSILON)
    module_index = jnp.maximum(section - 1, 0)
    module_block = module_weight[0]
    embed_scaling = lax.dynamic_index_in_dim(embed_gain, module_index, 0, keepdims=False).astype(
        jnp.float32
    )
    next_scaling = lax.dynamic_index_in_dim(
        hidden_gain, jnp.minimum(section, depth_count - 1), 0, keepdims=False
    ).astype(jnp.float32)
    out_scaling = out_gain[0].astype(jnp.float32)
    targets = lax.dynamic_slice_in_dim(token_ids, section + 1, TOK, 0) - shard_index * vocab_width
    whole_head = lax.all_gather(head_weight, "segment", axis=0, tiled=True)
    column_ids = lax.broadcasted_iota(jnp.int32, (micro_rows, vocab_width), 1)
    incoming = jnp.zeros((micro_rows, local_width), jnp.bfloat16)
    stored_tops = jnp.zeros((TOK,), jnp.float32)
    stored_totals = jnp.ones((TOK,), jnp.float32)
    stored_picks = jnp.zeros((TOK,), jnp.float32)
    for moment in range(MICRO + sections - 1):
        micro_index = moment - section
        active = (micro_index >= 0) & (micro_index < MICRO)
        first_row = jnp.clip(micro_index, 0, MICRO - 1) * micro_rows
        own_rows = lax.dynamic_slice_in_dim(trunk_out, first_row, micro_rows, 0)
        embed_rows = lax.dynamic_slice_in_dim(embed_float, first_row + section, micro_rows, 0)
        embed_factor = lax.dynamic_slice_in_dim(embed_scale, first_row + section, micro_rows, 0)
        embed_normed = (embed_rows * embed_factor[:, None] * embed_scaling).astype(jnp.bfloat16)
        partial_value = jnp.dot(incoming, module_block[0], preferred_element_type=jnp.float32)
        partial_value = partial_value + jnp.dot(
            embed_normed, module_block[1], preferred_element_type=jnp.float32
        )
        leading = section == 0
        placed = lax.dynamic_update_slice_in_dim(
            jnp.zeros((micro_rows, D), jnp.float32),
            own_rows.astype(jnp.float32),
            shard_index * local_width,
            1,
        )
        full_rows = lax.psum(jnp.where(leading, placed, partial_value), "vocab").astype(
            jnp.bfloat16
        )
        rows_float = full_rows.astype(jnp.float32)
        inverse_rms = lax.rsqrt(jnp.mean(rows_float * rows_float, axis=1, keepdims=True) + EPSILON)
        head_input = (rows_float * inverse_rms * out_scaling).astype(jnp.bfloat16)
        own_columns = lax.dynamic_slice_in_dim(
            rows_float, shard_index * local_width, local_width, 1
        )
        passed = (own_columns * inverse_rms * next_scaling).astype(jnp.bfloat16)
        incoming = passed_along(passed, "segment", 1)
        logits = jnp.dot(head_input, whole_head, preferred_element_type=jnp.float32)
        row_targets = lax.dynamic_slice_in_dim(targets, first_row, micro_rows, 0)
        row_target = jnp.sum(jnp.where(column_ids == row_targets[:, None], logits, 0.0), axis=1)
        row_top = jnp.max(logits, axis=1)
        row_total = jnp.sum(jnp.exp(logits - row_top[:, None]), axis=1)
        stored_tops = jnp.where(
            active, lax.dynamic_update_slice_in_dim(stored_tops, row_top, first_row, 0), stored_tops
        )
        stored_totals = jnp.where(
            active,
            lax.dynamic_update_slice_in_dim(stored_totals, row_total, first_row, 0),
            stored_totals,
        )
        stored_picks = jnp.where(
            active,
            lax.dynamic_update_slice_in_dim(stored_picks, row_target, first_row, 0),
            stored_picks,
        )
    merged_tops, merged_totals, merged_picks = combined_all(
        (stored_tops, stored_totals, stored_picks), "vocab", merge_softmax
    )
    losses = merged_tops + jnp.log(merged_totals) - merged_picks
    return losses[None, :]


def solution(mesh):
    in_specs = (
        P(None, "vocab"),
        P(None, "vocab"),
        P(),
        P("segment", None, "vocab", None),
        P(None, "vocab"),
        P(None, "vocab"),
        P("segment", None),
        P("segment", "vocab"),
    )
    out_specs = P("segment", None)
    return jax.shard_map(
        per_device, mesh=mesh, in_specs=in_specs, out_specs=out_specs, check_vma=False
    )
```

profile of v0, /device:TPU:5, one launch (start us, length us, event | category | flops | bytes accessed | tf_op | source)
XLA Modules:
  0.0 644.5 jit_solution(13789716217223740814)
XLA Ops:
  7.7 13.8 %psum.56 = f32[164]{0:T(256)S(1)} all-reduce(f32[164]{0:T(256)S(1)} %multiply_reduce_fusion.6), channel_id=1, replica_groups=mesh['segment'=4,'vocab'=8] {'vocab'}, use_global_device_ids=true, to_apply=%region_1.0 | all-reduce | flops 164 | bytes 1312 | tf_op jit(solution)/shard_map/psum | solution.py:47
  21.6 7.5 %fusion.12 = f32[40,7168]{1,0:T(8,128)S(1)} fusion(bf16[1,2,896,7168]{3,2,1,0:T(8,128)(2,1)} %param.13, f32[164,896]{1,0:T(8,128)S(1)} %convert_element_type.133, s32[]{:T(128)S(6)} %select_n.352, f32[896]{0:T(1024)S(1)} %fusion.139, f32[40]{0:T(128)S(1)} %get-tuple-element.231), kind=kOutput, calls=%fused_computation.16 | convolution fusion | flops 513909760 | bytes 14139908 | tf_op jit(solution)/shard_map/dot_general | solution.py:74
  30.1 5.9 fusion.67
  36.1 56.9 %all-reduce.7 = bf16[40,7168]{1,0:T(8,128)(2,1)S(1)} all-reduce(f32[40,7168]{1,0:T(8,128)S(1)} %fusion.67), channel_id=1, replica_groups=mesh['segment'=4,'vocab'=8] {'vocab'}, use_global_device_ids=true, to_apply=%region_2.3 | all-reduce | flops 286720 | bytes 1720320 | tf_op jit(solution)/shard_map/psum | solution.py:84
  94.0 3.6 collective-permute-start
  98.8 1.0 copy-done.5
  99.9 8.2 %fusion.10 = f32[40,7168]{1,0:T(8,128)} fusion(bf16[1,2,896,7168]{3,2,1,0:T(8,128)(2,1)} %param.13, f32[164,896]{1,0:T(8,128)S(1)} %convert_element_type.133, s32[]{:T(128)S(6)} %select_n.360, f32[40]{0:T(128)S(1)} %get-tuple-element.230, f32[896]{0:T(1024)S(1)} %fusion.139), kind=kOutput, calls=%fused_computation.14 | convolution fusion | flops 513909760 | bytes 14139908 | tf_op jit(solution)/shard_map/dot_general | solution.py:74
  108.1 8.3 %fusion.8 = f32[40,7168]{1,0:T(8,128)} fusion(bf16[1,2,896,7168]{3,2,1,0:T(8,128)(2,1)} %param.13, f32[164,896]{1,0:T(8,128)S(1)} %convert_element_type.133, s32[]{:T(128)S(6)} %select_n.367, f32[40]{0:T(128)S(1)} %get-tuple-element.229, f32[896]{0:T(1024)S(1)} %fusion.139), kind=kOutput, calls=%fused_computation.12 | convolution fusion | flops 513909760 | bytes 14139908 | tf_op jit(solution)/shard_map/dot_general | solution.py:74
  116.3 8.3 %fusion.6 = f32[40,7168]{1,0:T(8,128)} fusion(bf16[1,2,896,7168]{3,2,1,0:T(8,128)(2,1)} %param.13, f32[164,896]{1,0:T(8,128)} %copy-done.15, s32[]{:T(128)S(6)} %select_n.374, f32[40]{0:T(128)S(1)} %get-tuple-element.228, f32[896]{0:T(1024)S(1)} %fusion.139), kind=kOutput, calls=%fused_computation.10 | convolution fusion | flops 513909760 | bytes 14139044 | tf_op jit(solution)/shard_map/dot_general | solution.py:74
  124.6 8.1 %fusion.4 = f32[40,7168]{1,0:T(8,128)} fusion(bf16[1,2,896,7168]{3,2,1,0:T(8,128)(2,1)} %param.13, f32[164,896]{1,0:T(8,128)S(1)} %copy-done.16, s32[]{:T(128)S(6)} %select_n.381, f32[40]{0:T(128)S(1)} %get-tuple-element.227, f32[896]{0:T(1024)S(1)} %fusion.139), kind=kOutput, calls=%fused_computation.8 | convolution fusion | flops 513909760 | bytes 14139908 | tf_op jit(solution)/shard_map/dot_general | solution.py:74
  132.8 3.4 fusion.2
  136.3 3.4 fusion
  139.6 1.1 broadcast.145.clone.3
  141.4 4.4 fusion.64
  145.8 57.9 %all-reduce.8 = bf16[40,7168]{1,0:T(8,128)(2,1)S(1)} all-reduce(f32[40,7168]{1,0:T(8,128)} %fusion.64), channel_id=1, replica_groups=mesh['segment'=4,'vocab'=8] {'vocab'}, use_global_device_ids=true, to_apply=%region_5.6 | all-reduce | flops 286720 | bytes 1720320 | tf_op jit(solution)/shard_map/psum | solution.py:84
  204.2 2.2 collective-permute-start.1
  206.6 3.8 collective-permute-done.1
  210.3 8.0 %fusion.61 = f32[40,7168]{1,0:T(8,128)} fusion(f32[40,7168]{1,0:T(8,128)S(1)} %copy-done.6, f32[40,7168]{1,0:T(8,128)S(1)} %copy-done.14, bf16[40,896]{1,0:T(8,128)(2,1)S(1)} %collective-permute-done.1, bf16[1,2,896,7168]{3,2,1,0:T(8,128)(2,1)} %param.13, pred[]{:T(512)S(6)} %eq.30), kind=kOutput, calls=%fused_computation.43 | convolution fusion | flops 514375680 | bytes 16357377 | tf_op jit(solution)/shard_map/dot_general | solution.py:73
  218.4 59.6 %all-reduce.9 = bf16[40,7168]{1,0:T(8,128)(2,1)S(1)} all-reduce(f32[40,7168]{1,0:T(8,128)} %fusion.61), channel_id=1, replica_groups=mesh['segment'=4,'vocab'=8] {'vocab'}, use_global_device_ids=true, to_apply=%region_8.9 | all-reduce | flops 286720 | bytes 1720320 | tf_op jit(solution)/shard_map/psum | solution.py:84
  278.4 1.9 collective-permute-start.2
  280.4 1.1 broadcast.145.clone.5
  282.1 2.3 collective-permute-done.2
  284.4 8.0 %fusion.58 = f32[40,7168]{1,0:T(8,128)} fusion(f32[40,7168]{1,0:T(8,128)} %convert_dynamic-update-slice_fusion.3, f32[40,7168]{1,0:T(8,128)S(1)} %copy-done.13, bf16[40,896]{1,0:T(8,128)(2,1)S(1)} %collective-permute-done.2, bf16[1,2,896,7168]{3,2,1,0:T(8,128)(2,1)} %param.13, pred[]{:T(512)S(6)} %eq.30), kind=kOutput, calls=%fused_computation.42 | convolution fusion | flops 514375680 | bytes 16357377 | tf_op jit(solution)/shard_map/dot_general | solution.py:73
  292.4 58.2 %all-reduce.10 = bf16[40,7168]{1,0:T(8,128)(2,1)S(1)} all-reduce(f32[40,7168]{1,0:T(8,128)} %fusion.58), channel_id=1, replica_groups=mesh['segment'=4,'vocab'=8] {'vocab'}, use_global_device_ids=true, to_apply=%region_11.12 | all-reduce | flops 286720 | bytes 1720320 | tf_op jit(solution)/shard_map/psum | solution.py:84
  351.1 2.1 collective-permute-start.3
  353.3 3.9 collective-permute-done.3
  357.2 8.0 %fusion.55 = f32[40,7168]{1,0:T(8,128)} fusion(f32[40,7168]{1,0:T(8,128)S(1)} %copy-done.8, f32[40,7168]{1,0:T(8,128)S(1)} %copy-done.12, bf16[40,896]{1,0:T(8,128)(2,1)S(1)} %collective-permute-done.3, bf16[1,2,896,7168]{3,2,1,0:T(8,128)(2,1)} %param.13, pred[]{:T(512)S(6)} %eq.30), kind=kOutput, calls=%fused_computation.41 | convolution fusion | flops 514375680 | bytes 16357377 | tf_op jit(solution)/shard_map/dot_general | solution.py:73
  365.3 59.4 %all-reduce.11 = bf16[40,7168]{1,0:T(8,128)(2,1)S(1)} all-reduce(f32[40,7168]{1,0:T(8,128)} %fusion.55), channel_id=1, replica_groups=mesh['segment'=4,'vocab'=8] {'vocab'}, use_global_device_ids=true, to_apply=%region_14.15 | all-reduce | flops 286720 | bytes 1720320 | tf_op jit(solution)/shard_map/psum | solution.py:84
  425.1 1.9 collective-permute-start.4
  427.1 4.0 collective-permute-done.4
  431.1 8.0 %fusion.52 = f32[40,7168]{1,0:T(8,128)} fusion(f32[40,7168]{1,0:T(8,128)} %convert_dynamic-update-slice_fusion.1, f32[40,7168]{1,0:T(8,128)S(1)} %copy-done.11, bf16[40,896]{1,0:T(8,128)(2,1)S(1)} %collective-permute-done.4, bf16[1,2,896,7168]{3,2,1,0:T(8,128)(2,1)} %param.13, pred[]{:T(512)S(6)} %eq.30), kind=kOutput, calls=%fused_computation.40 | convolution fusion | flops 514375680 | bytes 16357377 | tf_op jit(solution)/shard_map/dot_general | solution.py:73
  439.1 58.8 %all-reduce.12 = bf16[40,7168]{1,0:T(8,128)(2,1)} all-reduce(f32[40,7168]{1,0:T(8,128)} %fusion.52), channel_id=1, replica_groups=mesh['segment'=4,'vocab'=8] {'vocab'}, use_global_device_ids=true, to_apply=%region_17.18 | all-reduce | flops 286720 | bytes 1720320 | tf_op jit(solution)/shard_map/psum | solution.py:84
  497.9 1.3 convert_element_type.302
  499.5 2.1 collective-permute-start.5
  501.7 3.7 collective-permute-done.5
  505.5 8.3 %fusion.49 = f32[40,7168]{1,0:T(8,128)} fusion(f32[40,7168]{1,0:T(8,128)S(1)} %copy-done.10, f32[40,7168]{1,0:T(8,128)} %fusion, bf16[40,896]{1,0:T(8,128)(2,1)S(1)} %collective-permute-done.5, bf16[1,2,896,7168]{3,2,1,0:T(8,128)(2,1)} %param.13, pred[]{:T(512)S(6)} %eq.30), kind=kOutput, calls=%fused_computation.39 | convolution fusion | flops 514375680 | bytes 16357377 | tf_op jit(solution)/shard_map/dot_general | solution.py:73
  513.8 59.9 %all-reduce.13 = bf16[40,7168]{1,0:T(8,128)(2,1)} all-reduce(f32[40,7168]{1,0:T(8,128)} %fusion.49), channel_id=1, replica_groups=mesh['segment'=4,'vocab'=8] {'vocab'}, use_global_device_ids=true, to_apply=%region_20.21 | all-reduce | flops 286720 | bytes 1720320 | tf_op jit(solution)/shard_map/psum | solution.py:84
  573.6 1.3 fusion.84
  574.9 8.1 %fusion.172 = (f32[40]{0:T(128)S(1)}, f32[40,1024]{1,0:T(8,128)S(1)}) fusion(bf16[7168,1024]{1,0:T(8,128)(2,1)} %all-gather.5.cloned.1.call-done, f32[7168]{0:T(1024)S(1)} %bitcast.105, f32[40]{0:T(128)S(1)} %add_rsqrt_fusion.7, bf16[40,7168]{1,0:T(8,128)(2,1)S(1)} %all-reduce.7), kind=kOutput, calls=%fused_computation.245 | convolution fusion | flops 588390336 | bytes 15446336 | tf_op jit(solution)/shard_map/dot_general | solution.py:95
  584.3 2.9 fusion.173
  587.6 2.9 fusion.175
  590.4 2.9 fusion.174
  594.2 2.9 fusion.177
  597.0 2.9 fusion.176
  600.5 2.9 fusion.178
  603.9 11.1 %all-gather.2 = f32[8,1,160]{2,1,0:T(1,128)S(1)} all-gather(f32[1,1,160]{2,1,0:T(1,128)S(1)} %select_n.451), channel_id=1, replica_groups=mesh['segment'=4,'vocab'=8] {'vocab'}, dimensions={0}, use_global_device_ids=true | all-gather | bytes 5760 | tf_op jit(solution)/shard_map/all_gather | solution.py:21
  615.9 9.6 %all-gather.1 = f32[8,1,160]{2,1,0:T(1,128)S(1)} all-gather(f32[1,1,160]{2,1,0:T(1,128)S(1)} %select_n.450), channel_id=1, replica_groups=mesh['segment'=4,'vocab'=8] {'vocab'}, dimensions={0}, use_global_device_ids=true | all-gather | bytes 5760 | tf_op jit(solution)/shard_map/all_gather | solution.py:21
  626.7 9.3 %all-gather = f32[8,1,160]{2,1,0:T(1,128)S(1)} all-gather(f32[1,1,160]{2,1,0:T(1,128)S(1)} %select_n.449), channel_id=1, replica_groups=mesh['segment'=4,'vocab'=8] {'vocab'}, dimensions={0}, use_global_device_ids=true | all-gather | bytes 5760 | tf_op jit(solution)/shard_map/all_gather | solution.py:21
  (176 shorter events, 15.3 us)
Async XLA Ops:
  6.5 1.0 copy-start.17
  6.5 568.4 %all-gather.5.cloned.1.call-start = ((), (), s32[]{:S(2)}) async-start(), calls=%async_computation | async-start | bytes 18350080 | tf_op jit(solution)/shard_map/all_gather | solution.py:59
  7.3 14.3 %copy-start.20 = (bf16[3,896]{1,0:T(4,128)(2,1)S(1)}, bf16[3,896]{1,0:T(4,128)(2,1)}, u32[]{:S(2)}) copy-start(bf16[3,896]{1,0:T(4,128)(2,1)} %param.15) | copy-start | bytes 16132
  7.7 100.4 %copy-start.15 = (f32[164,896]{1,0:T(8,128)}, f32[164,896]{1,0:T(8,128)S(1)}, u32[]{:S(2)}) copy-start(f32[164,896]{1,0:T(8,128)S(1)} %convert_element_type.133) | copy-start | bytes 1763332
  29.1 1.0 copy-start.18
  92.9 0.7 copy-start.21
  93.0 4.7 copy-start.19
  94.0 47.4 %collective-permute-start = (bf16[40,896]{1,0:T(8,128)(2,1)S(1)}, bf16[40,896]{1,0:T(8,128)(2,1)S(1)}, u32[]{:S(2)}, u32[]{:S(2)}) collective-permute-start(bf16[40,896]{1,0:T(8,128)(2,1)S(1)} %multiply_convert_fusion.23), channel_id=1, source_target_pairs={{0,8},{8,16},{16,24},{1,9},{9,17},{17,25},{2,10},{10,18},{18,26},{... | collective-permute-start | bytes 215048 | tf_op jit(solution)/shard_map/ppermute | solution.py:17
  97.8 1.0 copy-start.4
  98.8 1.0 copy-start.5
  99.9 32.9 %slice-start = ((s8[25690112]{0:T(1024)(128)(4,1)}), s8[4194304]{0:T(1024)(128)(4,1)S(1)}, s32[]{:S(2)}) async-start(s8[25690112]{0:T(1024)(128)(4,1)} %bitcast.103), calls=%async_computation.1 | async-start | bytes 8388608
  99.9 32.9 %slice-start.1 = ((s8[25690112]{0:T(1024)(128)(4,1)}), s8[4194304]{0:T(1024)(128)(4,1)S(1)}, s32[]{:S(2)}) async-start(s8[25690112]{0:T(1024)(128)(4,1)} %bitcast.103), calls=%async_computation.2 | async-start | bytes 8388608
  108.1 24.7 %slice-start.2 = ((s8[25690112]{0:T(1024)(128)(4,1)}), s8[4194304]{0:T(1024)(128)(4,1)S(1)}, s32[]{:S(2)}) async-start(s8[25690112]{0:T(1024)(128)(4,1)} %bitcast.103), calls=%async_computation.3 | async-start | bytes 8388608
  108.1 24.7 %slice-start.3 = ((s8[25690112]{0:T(1024)(128)(4,1)}), s8[4194304]{0:T(1024)(128)(4,1)S(1)}, s32[]{:S(2)}) async-start(s8[25690112]{0:T(1024)(128)(4,1)} %bitcast.103), calls=%async_computation.4 | async-start | bytes 8388608
  116.3 8.3 %copy-start.16 = (f32[164,896]{1,0:T(8,128)S(1)}, f32[164,896]{1,0:T(8,128)}, u32[]{:S(2)}) copy-start(f32[164,896]{1,0:T(8,128)} %copy-done.15) | copy-start | bytes 1763332
  116.3 16.5 %slice-start.4 = ((s8[25690112]{0:T(1024)(128)(4,1)}), s8[4194304]{0:T(1024)(128)(4,1)S(1)}, s32[]{:S(2)}) async-start(s8[25690112]{0:T(1024)(128)(4,1)} %bitcast.103), calls=%async_computation.5 | async-start | bytes 8388608
  116.3 16.5 %slice-start.5 = ((s8[25690112]{0:T(1024)(128)(4,1)}), s8[4194304]{0:T(1024)(128)(4,1)S(1)}, s32[]{:S(2)}) async-start(s8[25690112]{0:T(1024)(128)(4,1)} %bitcast.103), calls=%async_computation.6 | async-start | bytes 8388608
  124.6 8.2 %slice-start.6 = ((s8[25690112]{0:T(1024)(128)(4,1)}), s8[524288]{0:T(1024)(128)(4,1)S(1)}, s32[]{:S(2)}) async-start(s8[25690112]{0:T(1024)(128)(4,1)} %bitcast.103), calls=%async_computation.7 | async-start | bytes 1048576
  203.7 6.6 %copy-start.14 = (f32[40,7168]{1,0:T(8,128)S(1)}, f32[40,7168]{1,0:T(8,128)}, u32[]{:S(2)}) copy-start(f32[40,7168]{1,0:T(8,128)} %fusion.8) | copy-start | bytes 3440644
  203.8 6.5 %copy-start.6 = (f32[40,7168]{1,0:T(8,128)S(1)}, f32[40,7168]{1,0:T(8,128)}, u32[]{:S(2)}) copy-start(f32[40,7168]{1,0:T(8,128)} %copy-done.5) | copy-start | bytes 3440644
  204.2 6.1 collective-permute-start.1
  206.5 3.8 copy-start.7
  278.1 6.3 copy-start.13
  278.4 6.0 collective-permute-start.2
  350.7 6.6 %copy-start.12 = (f32[40,7168]{1,0:T(8,128)S(1)}, f32[40,7168]{1,0:T(8,128)}, u32[]{:S(2)}) copy-start(f32[40,7168]{1,0:T(8,128)} %fusion.4) | copy-start | bytes 3440644
  350.8 6.5 %copy-start.8 = (f32[40,7168]{1,0:T(8,128)S(1)}, f32[40,7168]{1,0:T(8,128)}, u32[]{:S(2)}) copy-start(f32[40,7168]{1,0:T(8,128)} %copy-done.7) | copy-start | bytes 3440644
  351.1 6.1 collective-permute-start.3
  353.3 3.9 copy-start.9
  424.6 2.4 copy-start.22
  424.6 6.4 copy-start.11
  425.1 6.0 collective-permute-start.4
  497.9 1.3 copy-start.1
  497.9 7.6 %copy-start.10 = (f32[40,7168]{1,0:T(8,128)S(1)}, f32[40,7168]{1,0:T(8,128)}, u32[]{:S(2)}) copy-start(f32[40,7168]{1,0:T(8,128)} %copy-done.9) | copy-start | bytes 3440644
  499.5 6.0 collective-permute-start.5
  574.9 9.3 %copy-start = (bf16[7168,1024]{1,0:T(8,128)(2,1)S(1)}, bf16[7168,1024]{1,0:T(8,128)(2,1)}, u32[]{:S(2)}) copy-start(bf16[7168,1024]{1,0:T(8,128)(2,1)} %all-gather.5.cloned.1.call-done) | copy-start | bytes 44040196
  590.4 3.7 copy-start.2
  597.0 3.5 copy-start.3
Sparse Core Ops, SparseCore 0:
  9.2 141.4 all-gather.4
where the time goes:
time: 648 us; the launch traced here: 644 us
  blocking collectives  454 us (70%)
  matrix products  123 us (19%)
  waiting for transfers between devices  18.4 us (3%)
  between operations  14.6 us (2%)
  starting transfers between devices  13.8 us (2%)
  other arithmetic  11.8 us (2%)
  local copies, waits for them, and re-layouts  7.92 us (1%)
    psum x7, blocking collectives, per_device(): lax.psum(jnp.where(leading, placed, partial_value), 'vocab')  411 us
    dot_general x7, matrix products, per_device(): jnp.dot(incoming, module_block[0], preferred_element_type=jnp.float32)  50.8 us
    dot_general x7, matrix products, per_device(): jnp.dot(embed_normed, module_block[1], preferred_element_type=jnp.float32)  47.2 us
    all_gather x3, blocking collectives, combined_all(): everything = jax.tree.map(lambda part: lax.all_gather(part, axis), shard)  30.1 us
    dot_general x7, matrix products, per_device(): logits = jnp.dot(head_input, whole_head, preferred_element_type=jnp.float32)  25.3 us
    ppermute x6, waiting for transfers between devices, passed_along(): return lax.ppermute(block, axis, route)  17.6 us
    ppermute x6, starting transfers between devices, passed_along(): return lax.ppermute(block, axis, route)  13.8 us
    psum x1, blocking collectives, per_device(): lax.psum(jnp.sum(embed_float * embed_float, axis=1), 'vocab')  13.8 us
  transfers between devices with their start and end apart: 7, of which 5 were waited for; matrix products, arithmetic and copies ran while one was open for 17% of the time, Pallas kernels for 0%

commit v1 on v0

v1 whole, which is shorter than its diff:
```python
import jax
import jax.numpy as jnp
from jax import lax
from jax.sharding import PartitionSpec as P

EPSILON = 1e-06
CORES = 2
BOTH = ("segment", "vocab")
WIRE = jnp.float16


class Grid:
    def __init__(self):
        self.sections = lax.axis_size("segment")
        self.shards = lax.axis_size("vocab")
        self.chips = self.shards // CORES
        self.section = lax.axis_index("segment")
        self.shard = lax.axis_index("vocab")
        self.chip = self.shard // CORES
        self.core = self.shard % CORES

    def send(self, block, target, sources=None):
        pairs = []
        for s in range(self.sections) if sources is None else sources:
            for z in range(self.chips):
                for c in range(CORES):
                    ts, tz, tc = target(s, z, c)
                    pairs.append((s * self.shards + z * CORES + c, ts * self.shards + tz * CORES + tc))
        return lax.ppermute(block, BOTH, pairs)

    def swap_core(self, block):
        return self.send(block, lambda s, z, c: (s, z, 1 - c))

    def swap_chip(self, block, d):
        return self.send(block, lambda s, z, c: (s, z ^ d, c))

    def swap_section(self, block, d):
        return self.send(block, lambda s, z, c: (s ^ d, z, c))

    def combine(self, value, merge):
        value = merge(value, self.swap_core(value))
        values = [value] + [self.swap_chip(value, d) for d in range(1, self.chips)]
        while len(values) > 1:
            values = [merge(a, b) for a, b in zip(values[0::2], values[1::2])]
        return values[0]


def merge_softmax(a, b):
    top = jnp.maximum(a[0], b[0])
    total = a[1] * jnp.exp(a[0] - top) + b[1] * jnp.exp(b[0] - top)
    return jnp.stack([top, total, a[2] + b[2]])


def per_device(
    trunk_out, embeds, token_ids, module_weight, hidden_gain, embed_gain, out_gain, head_weight
):
    grid = Grid()
    sections, chips, section, chip, core = grid.sections, grid.chips, grid.section, grid.chip, grid.core
    tokens, width = trunk_out.shape
    whole_width = module_weight.shape[3]
    vocab_width = head_weight.shape[1]
    depth_count = hidden_gain.shape[0]
    add = lambda a, b: a + b

    def squares(rows):
        return jnp.sum(rows * rows, axis=1)

    def scale_of(total):
        return lax.rsqrt(total / whole_width + EPSILON)

    hidden = trunk_out.astype(jnp.float32)
    embed_rows = lax.dynamic_slice_in_dim(embeds, section, tokens, 0).astype(jnp.float32)
    first = grid.combine(jnp.stack([squares(hidden), squares(embed_rows)]), add)
    scale = scale_of(first[0])
    embed_scale = scale_of(first[1])

    module_index = jnp.maximum(section - 1, 0)
    own_embed_gain = lax.dynamic_index_in_dim(embed_gain, module_index, 0, keepdims=False).astype(jnp.float32)
    own_hidden_gain = lax.dynamic_index_in_dim(hidden_gain, module_index, 0, keepdims=False).astype(jnp.float32)
    gain_slice = lax.dynamic_slice_in_dim(out_gain, grid.shard * width, width, 1)
    out_scaling = grid.send(gain_slice, lambda s, z, c: ((s + 1) % sections, z, c))[0].astype(jnp.float32)

    embed_part = (
        jnp.dot(
            (embed_rows * own_embed_gain).astype(jnp.bfloat16),
            module_weight[0, 1],
            preferred_element_type=jnp.float32,
        )
        * embed_scale[:, None]
    )
    for k in range(1, depth_count + 1):
        product = jnp.dot(
            (hidden * own_hidden_gain).astype(jnp.bfloat16),
            module_weight[0, 0],
            preferred_element_type=jnp.float32,
        )
        partial = product * scale[:, None] + embed_part
        blocks = [partial[:, j * width : (j + 1) * width] for j in range(grid.shards)]
        even = jnp.stack(blocks[0::2])
        odd = jnp.stack(blocks[1::2])
        mine = jnp.where(core == 0, even, odd)
        theirs = jnp.where(core == 0, odd, even).astype(WIRE)
        paired = (mine + grid.swap_core(theirs).astype(jnp.float32)).astype(WIRE)
        received = []
        for d in reversed(range(chips)):
            block = lax.dynamic_index_in_dim(paired, chip ^ d, 0, keepdims=False)
            received.append(
                grid.send(block, lambda s, z, c: ((s + 1) % sections, z ^ d, c), sources=(k,))
            )
        total = sum(part.astype(jnp.float32) for part in received)
        total = total.astype(jnp.bfloat16).astype(jnp.float32)
        arrived = section == (k + 1) % sections
        hidden = jnp.where(arrived, total, hidden)
        scale = jnp.where(arrived, scale_of(grid.combine(squares(hidden)[None], add)[0]), scale)

    head_input = (hidden * scale[:, None] * out_scaling).astype(jnp.bfloat16)
    group = chips // sections
    turned = grid.send(head_input, lambda a, z, c: (z // group, a * group + z % group, c))
    spread = jnp.zeros((chips, tokens, width), jnp.bfloat16)
    pieces = [turned] + [grid.swap_chip(turned, d) for d in range(1, chips)]
    for d in range(chips):
        spread = lax.dynamic_update_index_in_dim(spread, pieces[d], chip ^ d, 0)
    other = grid.swap_core(spread)
    even = jnp.where(core == 0, spread, other).reshape(sections, group, tokens, width)
    odd = jnp.where(core == 0, other, spread).reshape(sections, group, tokens, width)
    logits = 0.0
    for r in range(group):
        for c, half in enumerate((even, odd)):
            first_row = (r * CORES + c) * width
            logits = logits + jnp.dot(
                half[:, r].reshape(sections * tokens, width),
                head_weight[first_row : first_row + width],
                preferred_element_type=jnp.float32,
            )
    logits = logits.reshape(sections, tokens, vocab_width)

    def of_depth(values, k):
        return lax.dynamic_index_in_dim(values, (k + 1) % sections, 0, keepdims=False)

    sent = logits.astype(WIRE)
    rows = of_depth(logits, section)
    for d in reversed(range(1, sections)):
        rows = rows + grid.swap_section(of_depth(sent, section ^ d), d).astype(jnp.float32)
    targets = lax.dynamic_slice_in_dim(token_ids, section + 1, tokens, 0) - grid.shard * vocab_width
    column_ids = lax.broadcasted_iota(jnp.int32, (tokens, vocab_width), 1)
    pick = jnp.sum(jnp.where(column_ids == targets[:, None], rows, 0.0), axis=1)
    top = jnp.max(rows, axis=1)
    total = jnp.sum(jnp.exp(rows - top[:, None]), axis=1)
    top, total, pick = grid.combine(jnp.stack([top, total, pick]), merge_softmax)
    return (top + jnp.log(total) - pick)[None, :]


def solution(mesh):
    in_specs = (
        P(None, "vocab"),
        P(None, "vocab"),
        P(),
        P("segment", None, "vocab", None),
        P(None, "vocab"),
        P(None, "vocab"),
        P("segment", None),
        P("segment", "vocab"),
    )
    out_specs = P("segment", None)
    return jax.shard_map(
        per_device, mesh=mesh, in_specs=in_specs, out_specs=out_specs, check_vma=False
    )
```

time: 648 us -> 263 us (0.41)
  blocking collectives: 454 us -> 0 us
  waiting for transfers between devices: 18.4 us -> 117 us
  matrix products: 123 us -> 34.1 us
  starting transfers between devices: 13.8 us -> 93.8 us
  between operations: 14.6 us -> 0.49 us
    psum x8 -> x0, blocking collectives: 424 us -> none  [the longest x7 411 us: per_device(): lax.psum(jnp.where(leading, placed, partial_value), 'vocab')]
    ppermute x6 -> x44, waiting for transfers between devices: 17.6 us -> 117 us  [send(): return lax.ppermute(block, BOTH, pairs)]
    dot_general x21 -> x6, matrix products: 123 us -> 34.1 us  [the longest x3 24.9 us: per_device(): jnp.dot((hidden * own_hidden_gain).astype(jnp.bfloat16), module_weight[0,...]
    ppermute x6 -> x44, starting transfers between devices: 13.8 us -> 93.8 us  [send(): return lax.ppermute(block, BOTH, pairs)]
    all_gather x3 -> x0, blocking collectives: 30.1 us -> none  [combined_all(): everything = jax.tree.map(lambda part: lax.all_gather(part, axis), shard)]
  transfers between devices with their start and end apart: 7 -> 44, of which waited for: 5 -> 28; matrix products, arithmetic and copies ran while one was open for 17% -> 1% of each run, Pallas kernels for 0% -> 0%
where the time goes in v1:
time: 263 us; the launch traced here: 260 us
  waiting for transfers between devices  117 us (44%)
  starting transfers between devices  93.8 us (36%)
  matrix products  34.1 us (13%)
  other arithmetic  11.8 us (4%)
  local copies, waits for them, and re-layouts  3.01 us (1%)
    ppermute x44, waiting for transfers between devices, send(): return lax.ppermute(block, BOTH, pairs)  117 us
    ppermute x44, starting transfers between devices, send(): return lax.ppermute(block, BOTH, pairs)  93.8 us
    dot_general x3, matrix products, per_device(): jnp.dot((hidden * own_hidden_gain).astype(jnp.bfloat16), module_weight[0,...  24.9 us
    dot_general x1, matrix products, per_device(): jnp.dot((embed_rows * own_embed_gain).astype(jnp.bfloat16), module_weight...  6.22 us
  transfers between devices with their start and end apart: 44, of which 28 were waited for; matrix products, arithmetic and copies ran while one was open for 1% of the time, Pallas kernels for 0%

profile of v1, /device:TPU:5, one launch (start us, length us, event | category | flops | bytes accessed | tf_op | source)
XLA Modules:
  0.0 259.8 jit_solution(17074410445317186097)
XLA Ops:
  3.8 1.4 collective-permute-start.1
  5.2 2.3 collective-permute-start.2
  8.5 3.2 %collective-permute-done.3 = f32[2,160]{1,0:T(2,128)S(1)} collective-permute-done((f32[2,160]{1,0:T(2,128)S(1)}, f32[2,160]{1,0:T(2,128)S(1)}, u32[]{:S(2)}, u32[]{:S(2)}) %collective-permute-start.3) | collective-permute-done | bytes 1312 | tf_op jit(solution)/shard_map/ppermute | solution.py:29
  11.8 6.2 %fusion.30 = f32[160,7168]{1,0:T(8,128)S(1)} fusion(bf16[1,2,896,7168]{3,2,1,0:T(8,128)(2,1)} %param.11, f32[160]{0:T(256)S(1)} %bitcast.162, f32[896]{0:T(1024)S(1)} %get-tuple-element.62, bf16[164,896]{1,0:T(8,128)(2,1)} %param.9, s32[]{:T(128)S(6)} %select_n.187), kind=kOutput, calls=%fused_computation.18 | convolution fusion | flops 2056785920 | bytes 17723524 | tf_op jit(solution)/shard_map/dot_general | solution.py:84
  18.0 7.8 %fusion.15 = f32[160,7168]{1,0:T(8,128)S(1)} fusion(f32[160,7168]{1,0:T(8,128)S(1)} %fusion.30, bf16[1,2,896,7168]{3,2,1,0:T(8,128)(2,1)} %param.11, f32[160]{0:T(256)S(1)} %bitcast.158, bf16[160,896]{1,0:T(8,128)(2,1)S(1)} %copy-done.3, f32[896]{0:T(1024)S(1)} %get-tuple-element.61), kind=kOutput, calls=%fused_computation.13 | convolution fusion | flops 2057932800 | bytes 22311040 | tf_op jit(solution)/shard_map/dot_general | solution.py:92
  26.2 1.4 select_convert_fusion.2
  27.6 2.0 collective-permute-start.4
  29.6 2.8 %collective-permute-done.4 = f16[4,160,896]{2,1,0:T(8,128)(2,1)} collective-permute-done((f16[4,160,896]{2,1,0:T(8,128)(2,1)}, f16[4,160,896]{2,1,0:T(8,128)(2,1)}, u32[]{:S(2)}, u32[]{:S(2)}) %collective-permute-start.4) | collective-permute-done | bytes 1146912 | tf_op jit(solution)/shard_map/ppermute | solution.py:29
  32.4 2.1 add_convert_fusion.2
  34.7 1.3 collective-permute-start.5
  36.0 1.3 collective-permute-start.6
  39.9 8.4 %collective-permute-done.5 = f16[160,896]{1,0:T(8,128)(2,1)S(1)} collective-permute-done((f16[160,896]{1,0:T(8,128)(2,1)S(1)}, f16[160,896]{1,0:T(8,128)(2,1)S(1)}, u32[]{:S(2)}, u32[]{:S(2)}) %collective-permute-start.5) | collective-permute-done | bytes 286752 | tf_op jit(solution)/shard_map/ppermute | solution.py:29
  48.4 17.5 %collective-permute-done.6 = f16[160,896]{1,0:T(8,128)(2,1)S(1)} collective-permute-done((f16[160,896]{1,0:T(8,128)(2,1)S(1)}, f16[160,896]{1,0:T(8,128)(2,1)S(1)}, u32[]{:S(2)}, u32[]{:S(2)}) %collective-permute-start.6) | collective-permute-done | bytes 286752 | tf_op jit(solution)/shard_map/ppermute | solution.py:29
  65.8 1.7 collective-permute-done.8
  70.3 2.5 collective-permute-start.12
  72.7 1.8 collective-permute-done.12
  74.5 8.6 %fusion.21 = f32[160,7168]{1,0:T(8,128)S(1)} fusion(f32[160,7168]{1,0:T(8,128)} %copy-done.7, bf16[1,2,896,7168]{3,2,1,0:T(8,128)(2,1)} %param.11, f32[160]{0:T(256)S(1)} %broadcast_select_fusion.4, bf16[160,896]{1,0:T(8,128)(2,1)S(1)} %copy-done.4, bf16[160,896]{1,0:T(8,128)(2,1)S(1)} %get-tuple-element.16, f32[896]{0:T(1024)S(1)} %get-tuple-element.61, ...), kind=kOutput, calls=%fused_computation.15 | convolution fusion | flops 2058219520 | bytes 22597760 | tf_op jit(solution)/shard_map/dot_general | solution.py:92
  83.7 1.8 collective-permute-start.13
  85.5 2.4 collective-permute-done.13
  88.7 1.3 collective-permute-start.14
  90.0 1.3 collective-permute-start.15
  91.3 1.3 collective-permute-start.16
  92.6 1.5 collective-permute-start.17
  94.1 2.0 collective-permute-done.14
  96.1 6.2 %collective-permute-done.15 = f16[160,896]{1,0:T(8,128)(2,1)S(1)} collective-permute-done((f16[160,896]{1,0:T(8,128)(2,1)S(1)}, f16[160,896]{1,0:T(8,128)(2,1)S(1)}, u32[]{:S(2)}, u32[]{:S(2)}) %collective-permute-start.15) | collective-permute-done | bytes 286752 | tf_op jit(solution)/shard_map/ppermute | solution.py:29
  102.3 10.5 %collective-permute-done.16 = f16[160,896]{1,0:T(8,128)(2,1)S(1)} collective-permute-done((f16[160,896]{1,0:T(8,128)(2,1)S(1)}, f16[160,896]{1,0:T(8,128)(2,1)S(1)}, u32[]{:S(2)}, u32[]{:S(2)}) %collective-permute-start.16) | collective-permute-done | bytes 286752 | tf_op jit(solution)/shard_map/ppermute | solution.py:29
  115.0 4.6 %collective-permute-start.19 = (f32[1,160]{1,0:T(1,128)S(1)}, f32[1,160]{1,0:T(1,128)S(1)}, u32[]{:S(2)}, u32[]{:S(2)}) collective-permute-start(f32[1,160]{1,0:T(1,128)S(1)} %add.313), channel_id=1, source_target_pairs={{0,2},{1,3},{2,0},{3,1},{4,6},{5,7},{6,4},{7,5},{8,10},{9,11},{10,... | collective-permute-start | bytes 1928 | tf_op jit(solution)/shard_map/ppermute | solution.py:29
  119.6 2.1 collective-permute-start.21
  123.9 8.5 %fusion.27 = f32[160,7168]{1,0:T(8,128)S(1)} fusion(f32[160,7168]{1,0:T(8,128)} %copy-done.7, bf16[1,2,896,7168]{3,2,1,0:T(8,128)(2,1)} %param.11, f32[160]{0:T(256)S(1)} %broadcast_select_fusion.3, f32[160,896]{1,0:T(8,128)S(1)} %get-tuple-element.14, f32[896]{0:T(1024)S(1)} %get-tuple-element.61), kind=kOutput, calls=%fused_computation.17 | convolution fusion | flops 2057789440 | bytes 22597760 | tf_op jit(solution)/shard_map/dot_general | solution.py:92
  133.1 1.8 collective-permute-start.22
  134.9 2.4 collective-permute-done.22
  140.7 7.1 %collective-permute-start.31 = (bf16[1,896]{1,0:T(2,128)(2,1)S(1)}, bf16[1,896]{1,0:T(2,128)(2,1)S(1)}, u32[]{:S(2)}, u32[]{:S(2)}) collective-permute-start(bf16[1,896]{1,0:T(2,128)(2,1)S(1)} %constant_dynamic-slice_fusion), channel_id=1, source_target_pairs={{0,8},{1,9},{2,10},{3,11},{4,12},{5,13},{6,14},{7,15},{8,16},{9,17... | collective-permute-start | bytes 5384 | tf_op jit(solution)/shard_map/ppermute | solution.py:29
  150.8 2.5 collective-permute-start.30
  153.3 1.7 collective-permute-done.30
  155.2 25.2 %collective-permute-start.32 = (bf16[160,896]{1,0:T(8,128)(2,1)S(1)}, bf16[160,896]{1,0:T(8,128)(2,1)S(1)}, u32[]{:S(2)}, u32[]{:S(2)}) collective-permute-start(bf16[160,896]{1,0:T(8,128)(2,1)S(1)} %multiply_convert_fusion), channel_id=1, source_target_pairs={{0,0},{1,1},{2,8},{3,9},{4,16},{5,17},{6,24},{7,25},{8,2},{9,3},{1... | collective-permute-start | bytes 860168 | tf_op jit(solution)/shard_map/ppermute | solution.py:29
  180.4 11.7 %collective-permute-done.32 = bf16[160,896]{1,0:T(8,128)(2,1)S(1)} collective-permute-done((bf16[160,896]{1,0:T(8,128)(2,1)S(1)}, bf16[160,896]{1,0:T(8,128)(2,1)S(1)}, u32[]{:S(2)}, u32[]{:S(2)}) %collective-permute-start.32) | collective-permute-done | bytes 286752 | tf_op jit(solution)/shard_map/ppermute | solution.py:29
  192.1 6.6 %collective-permute-start.34 = (bf16[160,896]{1,0:T(8,128)(2,1)S(1)}, bf16[160,896]{1,0:T(8,128)(2,1)S(1)}, u32[]{:S(2)}, u32[]{:S(2)}) collective-permute-start(bf16[160,896]{1,0:T(8,128)(2,1)S(1)} %collective-permute-done.32), channel_id=1, source_target_pairs={{0,4},{1,5},{2,6},{3,7},{4,0},{5,1},{6,2},{7,3},{8,12},{9,13},{10,... | collective-permute-start | bytes 860168 | tf_op jit(solution)/shard_map/ppermute | solution.py:29
  198.9 6.0 %collective-permute-done.34 = bf16[160,896]{1,0:T(8,128)(2,1)S(1)} collective-permute-done((bf16[160,896]{1,0:T(8,128)(2,1)S(1)}, bf16[160,896]{1,0:T(8,128)(2,1)S(1)}, u32[]{:S(2)}, u32[]{:S(2)}) %collective-permute-start.34) | collective-permute-done | bytes 286752 | tf_op jit(solution)/shard_map/ppermute | solution.py:29
  204.9 12.1 %collective-permute-done.35 = bf16[160,896]{1,0:T(8,128)(2,1)S(1)} collective-permute-done((bf16[160,896]{1,0:T(8,128)(2,1)S(1)}, bf16[160,896]{1,0:T(8,128)(2,1)S(1)}, u32[]{:S(2)}, u32[]{:S(2)}) %collective-permute-start.35) | collective-permute-done | bytes 286752 | tf_op jit(solution)/shard_map/ppermute | solution.py:29
  217.1 3.1 %collective-permute-start.36 = (bf16[4,160,896]{2,1,0:T(8,128)(2,1)S(1)}, bf16[4,160,896]{2,1,0:T(8,128)(2,1)S(1)}, u32[]{:S(2)}, u32[]{:S(2)}) collective-permute-start(bf16[4,160,896]{2,1,0:T(8,128)(2,1)S(1)} %bitcast_dynamic-update-slice_fusion), channel_id=1, source_target_pairs={{0,1},{1,0},{2,3},{3,2},{4,5},{5,4},{6,7},{7,6},{8,9},{9,8},{10,11... | collective-permute-start | bytes 3440648 | tf_op jit(solution)/shard_map/ppermute | solution.py:29
  220.2 2.4 collective-permute-done.36
  222.9 1.5 fusion.33
  224.4 1.5 fusion.37
  227.3 4.0 %collective-permute-start.37 = (f16[160,1024]{1,0:T(8,128)(2,1)}, f16[160,1024]{1,0:T(8,128)(2,1)S(1)}, u32[]{:S(2)}, u32[]{:S(2)}) collective-permute-start(f16[160,1024]{1,0:T(8,128)(2,1)} %get-tuple-element.43), channel_id=1, source_target_pairs={{0,24},{1,25},{2,26},{3,27},{4,28},{5,29},{6,30},{7,31},{8,16},{9,... | collective-permute-start | bytes 983048 | tf_op jit(solution)/shard_map/ppermute | solution.py:29
  231.7 7.6 %collective-permute-done.37 = f16[160,1024]{1,0:T(8,128)(2,1)S(1)} collective-permute-done((f16[160,1024]{1,0:T(8,128)(2,1)}, f16[160,1024]{1,0:T(8,128)(2,1)S(1)}, u32[]{:S(2)}, u32[]{:S(2)}) %collective-permute-start.37) | collective-permute-done | bytes 327712 | tf_op jit(solution)/shard_map/ppermute | solution.py:29
  239.3 7.4 %collective-permute-done.38 = f16[160,1024]{1,0:T(8,128)(2,1)S(1)} collective-permute-done((f16[160,1024]{1,0:T(8,128)(2,1)}, f16[160,1024]{1,0:T(8,128)(2,1)S(1)}, u32[]{:S(2)}, u32[]{:S(2)}) %collective-permute-start.38) | collective-permute-done | bytes 327712 | tf_op jit(solution)/shard_map/ppermute | solution.py:29
  249.7 5.2 %collective-permute-start.41 = (f32[3,160]{1,0:T(4,128)S(1)}, f32[3,160]{1,0:T(4,128)S(1)}, u32[]{:S(2)}, u32[]{:S(2)}) collective-permute-start(f32[3,160]{1,0:T(4,128)S(1)} %pad_maximum_fusion.7), channel_id=1, source_target_pairs={{0,2},{1,3},{2,0},{3,1},{4,6},{5,7},{6,4},{7,5},{8,10},{9,11},{10,... | collective-permute-start | bytes 5768 | tf_op jit(solution)/shard_map/ppermute | solution.py:29
  254.9 2.1 collective-permute-start.43
  (111 shorter events, 31.3 us)
Async XLA Ops:
  0.0 140.7 %copy-start = (bf16[1,7168]{1,0:T(2,128)(2,1)S(1)}, bf16[1,7168]{1,0:T(2,128)(2,1)}, u32[]{:S(2)}) copy-start(bf16[1,7168]{1,0:T(2,128)(2,1)} %param.14) | copy-start | bytes 43012
  2.3 1.6 collective-permute-start
  3.8 4.4 %collective-permute-start.1 = (f32[2,160]{1,0:T(2,128)S(1)}, f32[2,160]{1,0:T(2,128)S(1)}, u32[]{:S(2)}, u32[]{:S(2)}) collective-permute-start(f32[2,160]{1,0:T(2,128)S(1)} %fusion.74), channel_id=1, source_target_pairs={{0,2},{1,3},{2,0},{3,1},{4,6},{5,7},{6,4},{7,5},{8,10},{9,11},{10,... | collective-permute-start | bytes 3848 | tf_op jit(solution)/shard_map/ppermute | solution.py:29
  5.2 3.3 %collective-permute-start.2 = (f32[2,160]{1,0:T(2,128)S(1)}, f32[2,160]{1,0:T(2,128)S(1)}, u32[]{:S(2)}, u32[]{:S(2)}) collective-permute-start(f32[2,160]{1,0:T(2,128)S(1)} %fusion.74), channel_id=1, source_target_pairs={{0,4},{1,5},{2,6},{3,7},{4,0},{5,1},{6,2},{7,3},{8,12},{9,13},{10,... | collective-permute-start | bytes 3848 | tf_op jit(solution)/shard_map/ppermute | solution.py:29
  7.5 4.2 %collective-permute-start.3 = (f32[2,160]{1,0:T(2,128)S(1)}, f32[2,160]{1,0:T(2,128)S(1)}, u32[]{:S(2)}, u32[]{:S(2)}) collective-permute-start(f32[2,160]{1,0:T(2,128)S(1)} %fusion.74), channel_id=1, source_target_pairs={{0,6},{1,7},{2,4},{3,5},{4,2},{5,3},{6,0},{7,1},{8,14},{9,15},{10,... | collective-permute-start | bytes 3848 | tf_op jit(solution)/shard_map/ppermute | solution.py:29
  11.8 6.2 %copy-start.3 = (bf16[160,896]{1,0:T(8,128)(2,1)S(1)}, bf16[160,896]{1,0:T(8,128)(2,1)}, u32[]{:S(2)}) copy-start(bf16[160,896]{1,0:T(8,128)(2,1)} %param.8) | copy-start | bytes 860164
  18.0 7.8 %copy-start.7 = (f32[160,7168]{1,0:T(8,128)}, f32[160,7168]{1,0:T(8,128)S(1)}, u32[]{:S(2)}) copy-start(f32[160,7168]{1,0:T(8,128)S(1)} %fusion.30) | copy-start | bytes 13762564
  27.6 4.8 %collective-permute-start.4 = (f16[4,160,896]{2,1,0:T(8,128)(2,1)}, f16[4,160,896]{2,1,0:T(8,128)(2,1)}, u32[]{:S(2)}, u32[]{:S(2)}) collective-permute-start(f16[4,160,896]{2,1,0:T(8,128)(2,1)} %select_convert_fusion.2), channel_id=1, source_target_pairs={{0,1},{1,0},{2,3},{3,2},{4,5},{5,4},{6,7},{7,6},{8,9},{9,8},{10,11... | collective-permute-start | bytes 3440648 | tf_op jit(solution)/shard_map/ppermute | solution.py:29
  34.5 33.0 %copy-start.4 = (bf16[160,896]{1,0:T(8,128)(2,1)S(1)}, bf16[160,896]{1,0:T(8,128)(2,1)}, u32[]{:S(2)}) copy-start(bf16[160,896]{1,0:T(8,128)(2,1)} %param.8) | copy-start | bytes 860164
  34.7 13.6 %collective-permute-start.5 = (f16[160,896]{1,0:T(8,128)(2,1)S(1)}, f16[160,896]{1,0:T(8,128)(2,1)S(1)}, u32[]{:S(2)}, u32[]{:S(2)}) collective-permute-start(f16[160,896]{1,0:T(8,128)(2,1)S(1)} %get-tuple-element.54), channel_id=1, source_target_pairs={{8,22},{9,23},{10,20},{11,21},{12,18},{13,19},{14,16},{15,17}} | collective-permute-start | bytes 860168 | tf_op jit(solution)/shard_map/ppermute | solution.py:29
  36.0 29.8 %collective-permute-start.6 = (f16[160,896]{1,0:T(8,128)(2,1)S(1)}, f16[160,896]{1,0:T(8,128)(2,1)S(1)}, u32[]{:S(2)}, u32[]{:S(2)}) collective-permute-start(f16[160,896]{1,0:T(8,128)(2,1)S(1)} %get-tuple-element.57), channel_id=1, source_target_pairs={{8,20},{9,21},{10,22},{11,23},{12,16},{13,17},{14,18},{15,19}} | collective-permute-start | bytes 860168 | tf_op jit(solution)/shard_map/ppermute | solution.py:29
  37.3 28.5 %collective-permute-start.7 = (f16[160,896]{1,0:T(8,128)(2,1)S(1)}, f16[160,896]{1,0:T(8,128)(2,1)S(1)}, u32[]{:S(2)}, u32[]{:S(2)}) collective-permute-start(f16[160,896]{1,0:T(8,128)(2,1)S(1)} %get-tuple-element.56), channel_id=1, source_target_pairs={{8,18},{9,19},{10,16},{11,17},{12,22},{13,23},{14,20},{15,21}} | collective-permute-start | bytes 860168 | tf_op jit(solution)/shard_map/ppermute | solution.py:29
  38.6 28.9 %collective-permute-start.8 = (f16[160,896]{1,0:T(8,128)(2,1)S(1)}, f16[160,896]{1,0:T(8,128)(2,1)S(1)}, u32[]{:S(2)}, u32[]{:S(2)}) collective-permute-start(f16[160,896]{1,0:T(8,128)(2,1)S(1)} %get-tuple-element.55), channel_id=1, source_target_pairs={{8,16},{9,17},{10,18},{11,19},{12,20},{13,21},{14,22},{15,23}} | collective-permute-start | bytes 860168 | tf_op jit(solution)/shard_map/ppermute | solution.py:29
  67.8 1.4 collective-permute-start.9
  69.2 3.6 %collective-permute-start.10 = (f32[1,160]{1,0:T(1,128)S(1)}, f32[1,160]{1,0:T(1,128)S(1)}, u32[]{:S(2)}, u32[]{:S(2)}) collective-permute-start(f32[1,160]{1,0:T(1,128)S(1)} %add.303), channel_id=1, source_target_pairs={{0,2},{1,3},{2,0},{3,1},{4,6},{5,7},{6,4},{7,5},{8,10},{9,11},{10,... | collective-permute-start | bytes 1928 | tf_op jit(solution)/shard_map/ppermute | solution.py:29
  69.2 3.6 %collective-permute-start.11 = (f32[1,160]{1,0:T(1,128)S(1)}, f32[1,160]{1,0:T(1,128)S(1)}, u32[]{:S(2)}, u32[]{:S(2)}) collective-permute-start(f32[1,160]{1,0:T(1,128)S(1)} %add.303), channel_id=1, source_target_pairs={{0,4},{1,5},{2,6},{3,7},{4,0},{5,1},{6,2},{7,3},{8,12},{9,13},{10,... | collective-permute-start | bytes 1928 | tf_op jit(solution)/shard_map/ppermute | solution.py:29
  70.3 4.2 %collective-permute-start.12 = (f32[1,160]{1,0:T(1,128)S(1)}, f32[1,160]{1,0:T(1,128)S(1)}, u32[]{:S(2)}, u32[]{:S(2)}) collective-permute-start(f32[1,160]{1,0:T(1,128)S(1)} %add.303), channel_id=1, source_target_pairs={{0,6},{1,7},{2,4},{3,5},{4,2},{5,3},{6,0},{7,1},{8,14},{9,15},{10,... | collective-permute-start | bytes 1928 | tf_op jit(solution)/shard_map/ppermute | solution.py:29
  83.7 4.3 %collective-permute-start.13 = (f16[4,160,896]{2,1,0:T(8,128)(2,1)S(1)}, f16[4,160,896]{2,1,0:T(8,128)(2,1)S(1)}, u32[]{:S(2)}, u32[]{:S(2)}) collective-permute-start(f16[4,160,896]{2,1,0:T(8,128)(2,1)S(1)} %select_convert_fusion.1), channel_id=1, source_target_pairs={{0,1},{1,0},{2,3},{3,2},{4,5},{5,4},{6,7},{7,6},{8,9},{9,8},{10,11... | collective-permute-start | bytes 3440648 | tf_op jit(solution)/shard_map/ppermute | solution.py:29
  88.7 7.5 %collective-permute-start.14 = (f16[160,896]{1,0:T(8,128)(2,1)S(1)}, f16[160,896]{1,0:T(8,128)(2,1)S(1)}, u32[]{:S(2)}, u32[]{:S(2)}) collective-permute-start(f16[160,896]{1,0:T(8,128)(2,1)S(1)} %get-tuple-element.50), channel_id=1, source_target_pairs={{16,30},{17,31},{18,28},{19,29},{20,26},{21,27},{22,24},{23,25}} | collective-permute-start | bytes 860168 | tf_op jit(solution)/shard_map/ppermute | solution.py:29
  90.0 12.3 %collective-permute-start.15 = (f16[160,896]{1,0:T(8,128)(2,1)S(1)}, f16[160,896]{1,0:T(8,128)(2,1)S(1)}, u32[]{:S(2)}, u32[]{:S(2)}) collective-permute-start(f16[160,896]{1,0:T(8,128)(2,1)S(1)} %get-tuple-element.53), channel_id=1, source_target_pairs={{16,28},{17,29},{18,30},{19,31},{20,24},{21,25},{22,26},{23,27}} | collective-permute-start | bytes 860168 | tf_op jit(solution)/shard_map/ppermute | solution.py:29
  91.3 21.5 %collective-permute-start.16 = (f16[160,896]{1,0:T(8,128)(2,1)S(1)}, f16[160,896]{1,0:T(8,128)(2,1)S(1)}, u32[]{:S(2)}, u32[]{:S(2)}) collective-permute-start(f16[160,896]{1,0:T(8,128)(2,1)S(1)} %get-tuple-element.52), channel_id=1, source_target_pairs={{16,26},{17,27},{18,24},{19,25},{20,30},{21,31},{22,28},{23,29}} | collective-permute-start | bytes 860168 | tf_op jit(solution)/shard_map/ppermute | solution.py:29
  92.6 20.2 %collective-permute-start.17 = (f16[160,896]{1,0:T(8,128)(2,1)S(1)}, f16[160,896]{1,0:T(8,128)(2,1)S(1)}, u32[]{:S(2)}, u32[]{:S(2)}) collective-permute-start(f16[160,896]{1,0:T(8,128)(2,1)S(1)} %get-tuple-element.51), channel_id=1, source_target_pairs={{16,24},{17,25},{18,26},{19,27},{20,28},{21,29},{22,30},{23,31}} | collective-permute-start | bytes 860168 | tf_op jit(solution)/shard_map/ppermute | solution.py:29
  113.1 1.8 collective-permute-start.18
  115.0 6.7 %collective-permute-start.19 = (f32[1,160]{1,0:T(1,128)S(1)}, f32[1,160]{1,0:T(1,128)S(1)}, u32[]{:S(2)}, u32[]{:S(2)}) collective-permute-start(f32[1,160]{1,0:T(1,128)S(1)} %add.313), channel_id=1, source_target_pairs={{0,2},{1,3},{2,0},{3,1},{4,6},{5,7},{6,4},{7,5},{8,10},{9,11},{10,... | collective-permute-start | bytes 1928 | tf_op jit(solution)/shard_map/ppermute | solution.py:29
  119.6 3.3 %collective-permute-start.20 = (f32[1,160]{1,0:T(1,128)S(1)}, f32[1,160]{1,0:T(1,128)S(1)}, u32[]{:S(2)}, u32[]{:S(2)}) collective-permute-start(f32[1,160]{1,0:T(1,128)S(1)} %add.313), channel_id=1, source_target_pairs={{0,4},{1,5},{2,6},{3,7},{4,0},{5,1},{6,2},{7,3},{8,12},{9,13},{10,... | collective-permute-start | bytes 1928 | tf_op jit(solution)/shard_map/ppermute | solution.py:29
  119.6 4.2 %collective-permute-start.21 = (f32[1,160]{1,0:T(1,128)S(1)}, f32[1,160]{1,0:T(1,128)S(1)}, u32[]{:S(2)}, u32[]{:S(2)}) collective-permute-start(f32[1,160]{1,0:T(1,128)S(1)} %add.313), channel_id=1, source_target_pairs={{0,6},{1,7},{2,4},{3,5},{4,2},{5,3},{6,0},{7,1},{8,14},{9,15},{10,... | collective-permute-start | bytes 1928 | tf_op jit(solution)/shard_map/ppermute | solution.py:29
  133.1 4.3 %collective-permute-start.22 = (f16[4,160,896]{2,1,0:T(8,128)(2,1)S(1)}, f16[4,160,896]{2,1,0:T(8,128)(2,1)S(1)}, u32[]{:S(2)}, u32[]{:S(2)}) collective-permute-start(f16[4,160,896]{2,1,0:T(8,128)(2,1)S(1)} %select_convert_fusion), channel_id=1, source_target_pairs={{0,1},{1,0},{2,3},{3,2},{4,5},{5,4},{6,7},{7,6},{8,9},{9,8},{10,11... | collective-permute-start | bytes 3440648 | tf_op jit(solution)/shard_map/ppermute | solution.py:29
  138.0 9.9 %collective-permute-start.23 = (f16[160,896]{1,0:T(8,128)(2,1)S(1)}, f16[160,896]{1,0:T(8,128)(2,1)S(1)}, u32[]{:S(2)}, u32[]{:S(2)}) collective-permute-start(f16[160,896]{1,0:T(8,128)(2,1)S(1)} %get-tuple-element.46), channel_id=1, source_target_pairs={{24,6},{25,7},{26,4},{27,5},{28,2},{29,3},{30,0},{31,1}} | collective-permute-start | bytes 860168 | tf_op jit(solution)/shard_map/ppermute | solution.py:29
  138.6 9.2 %collective-permute-start.24 = (f16[160,896]{1,0:T(8,128)(2,1)S(1)}, f16[160,896]{1,0:T(8,128)(2,1)S(1)}, u32[]{:S(2)}, u32[]{:S(2)}) collective-permute-start(f16[160,896]{1,0:T(8,128)(2,1)S(1)} %get-tuple-element.49), channel_id=1, source_target_pairs={{24,4},{25,5},{26,6},{27,7},{28,0},{29,1},{30,2},{31,3}} | collective-permute-start | bytes 860168 | tf_op jit(solution)/shard_map/ppermute | solution.py:29
  139.3 8.5 %collective-permute-start.25 = (f16[160,896]{1,0:T(8,128)(2,1)S(1)}, f16[160,896]{1,0:T(8,128)(2,1)S(1)}, u32[]{:S(2)}, u32[]{:S(2)}) collective-permute-start(f16[160,896]{1,0:T(8,128)(2,1)S(1)} %get-tuple-element.48), channel_id=1, source_target_pairs={{24,2},{25,3},{26,0},{27,1},{28,6},{29,7},{30,4},{31,5}} | collective-permute-start | bytes 860168 | tf_op jit(solution)/shard_map/ppermute | solution.py:29
  140.0 7.9 %collective-permute-start.26 = (f16[160,896]{1,0:T(8,128)(2,1)S(1)}, f16[160,896]{1,0:T(8,128)(2,1)S(1)}, u32[]{:S(2)}, u32[]{:S(2)}) collective-permute-start(f16[160,896]{1,0:T(8,128)(2,1)S(1)} %get-tuple-element.47), channel_id=1, source_target_pairs={{24,0},{25,1},{26,2},{27,3},{28,4},{29,5},{30,6},{31,7}} | collective-permute-start | bytes 860168 | tf_op jit(solution)/shard_map/ppermute | solution.py:29
  140.7 12.5 %collective-permute-start.31 = (bf16[1,896]{1,0:T(2,128)(2,1)S(1)}, bf16[1,896]{1,0:T(2,128)(2,1)S(1)}, u32[]{:S(2)}, u32[]{:S(2)}) collective-permute-start(bf16[1,896]{1,0:T(2,128)(2,1)S(1)} %constant_dynamic-slice_fusion), channel_id=1, source_target_pairs={{0,8},{1,9},{2,10},{3,11},{4,12},{5,13},{6,14},{7,15},{8,16},{9,17... | collective-permute-start | bytes 5384 | tf_op jit(solution)/shard_map/ppermute | solution.py:29
  148.2 1.5 collective-permute-start.27
  149.7 3.6 %collective-permute-start.28 = (f32[1,160]{1,0:T(1,128)S(1)}, f32[1,160]{1,0:T(1,128)S(1)}, u32[]{:S(2)}, u32[]{:S(2)}) collective-permute-start(f32[1,160]{1,0:T(1,128)S(1)} %add.323), channel_id=1, source_target_pairs={{0,2},{1,3},{2,0},{3,1},{4,6},{5,7},{6,4},{7,5},{8,10},{9,11},{10,... | collective-permute-start | bytes 1928 | tf_op jit(solution)/shard_map/ppermute | solution.py:29
  149.7 3.6 %collective-permute-start.29 = (f32[1,160]{1,0:T(1,128)S(1)}, f32[1,160]{1,0:T(1,128)S(1)}, u32[]{:S(2)}, u32[]{:S(2)}) collective-permute-start(f32[1,160]{1,0:T(1,128)S(1)} %add.323), channel_id=1, source_target_pairs={{0,4},{1,5},{2,6},{3,7},{4,0},{5,1},{6,2},{7,3},{8,12},{9,13},{10,... | collective-permute-start | bytes 1928 | tf_op jit(solution)/shard_map/ppermute | solution.py:29
  150.8 4.2 %collective-permute-start.30 = (f32[1,160]{1,0:T(1,128)S(1)}, f32[1,160]{1,0:T(1,128)S(1)}, u32[]{:S(2)}, u32[]{:S(2)}) collective-permute-start(f32[1,160]{1,0:T(1,128)S(1)} %add.323), channel_id=1, source_target_pairs={{0,6},{1,7},{2,4},{3,5},{4,2},{5,3},{6,0},{7,1},{8,14},{9,15},{10,... | collective-permute-start | bytes 1928 | tf_op jit(solution)/shard_map/ppermute | solution.py:29
  155.2 36.9 %collective-permute-start.32 = (bf16[160,896]{1,0:T(8,128)(2,1)S(1)}, bf16[160,896]{1,0:T(8,128)(2,1)S(1)}, u32[]{:S(2)}, u32[]{:S(2)}) collective-permute-start(bf16[160,896]{1,0:T(8,128)(2,1)S(1)} %multiply_convert_fusion), channel_id=1, source_target_pairs={{0,0},{1,1},{2,8},{3,9},{4,16},{5,17},{6,24},{7,25},{8,2},{9,3},{1... | collective-permute-start | bytes 860168 | tf_op jit(solution)/shard_map/ppermute | solution.py:29
  192.1 6.7 %collective-permute-start.33 = (bf16[160,896]{1,0:T(8,128)(2,1)S(1)}, bf16[160,896]{1,0:T(8,128)(2,1)S(1)}, u32[]{:S(2)}, u32[]{:S(2)}) collective-permute-start(bf16[160,896]{1,0:T(8,128)(2,1)S(1)} %collective-permute-done.32), channel_id=1, source_target_pairs={{0,2},{1,3},{2,0},{3,1},{4,6},{5,7},{6,4},{7,5},{8,10},{9,11},{10,... | collective-permute-start | bytes 860168 | tf_op jit(solution)/shard_map/ppermute | solution.py:29
  192.1 12.8 %collective-permute-start.34 = (bf16[160,896]{1,0:T(8,128)(2,1)S(1)}, bf16[160,896]{1,0:T(8,128)(2,1)S(1)}, u32[]{:S(2)}, u32[]{:S(2)}) collective-permute-start(bf16[160,896]{1,0:T(8,128)(2,1)S(1)} %collective-permute-done.32), channel_id=1, source_target_pairs={{0,4},{1,5},{2,6},{3,7},{4,0},{5,1},{6,2},{7,3},{8,12},{9,13},{10,... | collective-permute-start | bytes 860168 | tf_op jit(solution)/shard_map/ppermute | solution.py:29
  198.7 18.4 %collective-permute-start.35 = (bf16[160,896]{1,0:T(8,128)(2,1)S(1)}, bf16[160,896]{1,0:T(8,128)(2,1)S(1)}, u32[]{:S(2)}, u32[]{:S(2)}) collective-permute-start(bf16[160,896]{1,0:T(8,128)(2,1)S(1)} %collective-permute-done.32), channel_id=1, source_target_pairs={{0,6},{1,7},{2,4},{3,5},{4,2},{5,3},{6,0},{7,1},{8,14},{9,15},{10,... | collective-permute-start | bytes 860168 | tf_op jit(solution)/shard_map/ppermute | solution.py:29
  217.1 5.6 %collective-permute-start.36 = (bf16[4,160,896]{2,1,0:T(8,128)(2,1)S(1)}, bf16[4,160,896]{2,1,0:T(8,128)(2,1)S(1)}, u32[]{:S(2)}, u32[]{:S(2)}) collective-permute-start(bf16[4,160,896]{2,1,0:T(8,128)(2,1)S(1)} %bitcast_dynamic-update-slice_fusion), channel_id=1, source_target_pairs={{0,1},{1,0},{2,3},{3,2},{4,5},{5,4},{6,7},{7,6},{8,9},{9,8},{10,11... | collective-permute-start | bytes 3440648 | tf_op jit(solution)/shard_map/ppermute | solution.py:29
  227.3 12.0 %collective-permute-start.37 = (f16[160,1024]{1,0:T(8,128)(2,1)}, f16[160,1024]{1,0:T(8,128)(2,1)S(1)}, u32[]{:S(2)}, u32[]{:S(2)}) collective-permute-start(f16[160,1024]{1,0:T(8,128)(2,1)} %get-tuple-element.43), channel_id=1, source_target_pairs={{0,24},{1,25},{2,26},{3,27},{4,28},{5,29},{6,30},{7,31},{8,16},{9,... | collective-permute-start | bytes 983048 | tf_op jit(solution)/shard_map/ppermute | solution.py:29
  231.3 15.4 %collective-permute-start.38 = (f16[160,1024]{1,0:T(8,128)(2,1)}, f16[160,1024]{1,0:T(8,128)(2,1)S(1)}, u32[]{:S(2)}, u32[]{:S(2)}) collective-permute-start(f16[160,1024]{1,0:T(8,128)(2,1)} %get-tuple-element.45), channel_id=1, source_target_pairs={{0,16},{1,17},{2,18},{3,19},{4,20},{5,21},{6,22},{7,23},{8,24},{9,... | collective-permute-start | bytes 983048 | tf_op jit(solution)/shard_map/ppermute | solution.py:29
  231.3 15.4 %collective-permute-start.39 = (f16[160,1024]{1,0:T(8,128)(2,1)}, f16[160,1024]{1,0:T(8,128)(2,1)}, u32[]{:S(2)}, u32[]{:S(2)}) collective-permute-start(f16[160,1024]{1,0:T(8,128)(2,1)} %get-tuple-element.44), channel_id=1, source_target_pairs={{0,8},{1,9},{2,10},{3,11},{4,12},{5,13},{6,14},{7,15},{8,0},{9,1},... | collective-permute-start | bytes 983048 | tf_op jit(solution)/shard_map/ppermute | solution.py:29
  248.3 1.4 collective-permute-start.40
  249.7 7.4 %collective-permute-start.41 = (f32[3,160]{1,0:T(4,128)S(1)}, f32[3,160]{1,0:T(4,128)S(1)}, u32[]{:S(2)}, u32[]{:S(2)}) collective-permute-start(f32[3,160]{1,0:T(4,128)S(1)} %pad_maximum_fusion.7), channel_id=1, source_target_pairs={{0,2},{1,3},{2,0},{3,1},{4,6},{5,7},{6,4},{7,5},{8,10},{9,11},{10,... | collective-permute-start | bytes 5768 | tf_op jit(solution)/shard_map/ppermute | solution.py:29
  254.9 3.4 %collective-permute-start.42 = (f32[3,160]{1,0:T(4,128)S(1)}, f32[3,160]{1,0:T(4,128)S(1)}, u32[]{:S(2)}, u32[]{:S(2)}) collective-permute-start(f32[3,160]{1,0:T(4,128)S(1)} %pad_maximum_fusion.7), channel_id=1, source_target_pairs={{0,4},{1,5},{2,6},{3,7},{4,0},{5,1},{6,2},{7,3},{8,12},{9,13},{10,... | collective-permute-start | bytes 5768 | tf_op jit(solution)/shard_map/ppermute | solution.py:29
  254.9 4.3 %collective-permute-start.43 = (f32[3,160]{1,0:T(4,128)S(1)}, f32[3,160]{1,0:T(4,128)S(1)}, u32[]{:S(2)}, u32[]{:S(2)}) collective-permute-start(f32[3,160]{1,0:T(4,128)S(1)} %pad_maximum_fusion.7), channel_id=1, source_target_pairs={{0,6},{1,7},{2,4},{3,5},{4,2},{5,3},{6,0},{7,1},{8,14},{9,15},{10,... | collective-permute-start | bytes 5768 | tf_op jit(solution)/shard_map/ppermute | solution.py:29
  (4 other events, 11.1 us)
